TPU v7x, 256 devices: a whole 4x4x8 slice. The times are simulated.
256 devices in a mesh: dp: 8 (over y, core), seq: 32 (over x, z).
Axes of the slice: x: 4, y: 4, z: 8, core: 2. Of those that a mesh axis runs over, the one named last changes fastest.
Arguments:
- token_ids: int32 [8, 4096], P('dp', 'seq'), may hold values from 0 to 255
- cotangent: bfloat16 [8, 4096, 768], P('dp', 'seq'), may hold values from -6 to 6
- table: bfloat16 [256, 768], replicated, may hold values from -12 to 12
- w_query: bfloat16 [768, 768], replicated, may hold values from -2 to 2
- w_key: bfloat16 [768, 768], replicated, may hold values from -2 to 2
- w_value: bfloat16 [768, 768], replicated, may hold values from -0.21875 to 0.21875
- w_out: bfloat16 [768, 768], replicated, may hold values from -0.21875 to 0.21875
- window: int32 [12], replicated, may hold values from 64 to 512, as said below
Outputs:
- grad_input: bfloat16 [8, 4096, 768], P('dp', 'seq')
- weight_grads: float32 [3072, 768], P('seq')
Inputs may be any that keep to these rules, and one draw needn't show every extreme that they name: Some head's window is exactly 512.
All inputs are finite; a program needn't handle non-finite values.
Results may differ from a plain program's by a relative error of at most 0.025.
Values may be sent and summed in bfloat16 or wider, within the bound.
A program may use at most 128 MiB of HBM per device.

v0:
```python
import jax
import jax.numpy as jnp
from jax import lax
from jax.sharding import PartitionSpec as P

HEADS = 12
HEAD_DIM = 64
WINDOW = 512
EPSILON = 1e-05


def shifted(block, axis, distance):
    devices = range(lax.axis_size(axis))
    route = [(i - distance, i) for i in devices if i - distance in devices]
    return lax.ppermute(block, axis, route)


def rotate(values, positions):
    row_count = values.shape[0]
    shaped = values.reshape(row_count, -1, HEAD_DIM)
    middle = HEAD_DIM // 2
    frequency = 10000.0 ** (-2.0 * jnp.arange(middle, dtype=jnp.float32) / HEAD_DIM)
    angles = positions.astype(jnp.float32)[:, None] * frequency[None, :]
    cosine = jnp.cos(angles)[:, None, :]
    sine_part = jnp.sin(angles)[:, None, :]
    former = shaped[..., :middle]
    latter = shaped[..., middle:]
    turned = jnp.concatenate(
        [former * cosine - latter * sine_part, latter * cosine + former * sine_part], axis=-1
    )
    return turned.reshape(row_count, -1)


def unrotate(values, positions):
    row_count = values.shape[0]
    shaped = values.reshape(row_count, -1, HEAD_DIM)
    middle = HEAD_DIM // 2
    frequency = 10000.0 ** (-2.0 * jnp.arange(middle, dtype=jnp.float32) / HEAD_DIM)
    angles = positions.astype(jnp.float32)[:, None] * frequency[None, :]
    cosine = jnp.cos(angles)[:, None, :]
    sine_part = jnp.sin(angles)[:, None, :]
    former = shaped[..., :middle]
    latter = shaped[..., middle:]
    turned = jnp.concatenate(
        [former * cosine + latter * sine_part, latter * cosine - former * sine_part], axis=-1
    )
    return turned.reshape(row_count, -1)


def tdot(left, right):
    return lax.dot_general(
        left, right, (((0,), (0,)), ((), ())), preferred_element_type=jnp.float32
    )


def ndot(left, right):
    return lax.dot_general(
        left, right, (((1,), (1,)), ((), ())), preferred_element_type=jnp.float32
    )


def embed_rows(byte_ids, table):
    onehot = (byte_ids[:, None] == jnp.arange(table.shape[0], dtype=jnp.int32)[None, :]).astype(
        jnp.bfloat16
    )
    return jnp.dot(onehot, table, preferred_element_type=jnp.float32).astype(jnp.bfloat16)


def normalize(embedded):
    widened = embedded.astype(jnp.float32)
    inv_rms = lax.rsqrt(jnp.mean(widened * widened, axis=1, keepdims=True) + EPSILON)
    return (widened, inv_rms, (widened * inv_rms).astype(jnp.bfloat16))


def keys_values(normed, positions, w_key, w_value):
    key_rows = rotate(jnp.dot(normed, w_key, preferred_element_type=jnp.float32), positions).astype(
        jnp.bfloat16
    )
    value_rows = jnp.dot(normed, w_value, preferred_element_type=jnp.float32).astype(jnp.bfloat16)
    return (key_rows, value_rows)


def head_group(
    query_heads, key_heads, value_heads, grad_heads, group_window, own_pos, key_pos, score_scale
):
    distance = own_pos[:, None] - key_pos[None, :]
    allowed = (
        (distance[None] >= 0)
        & (distance[None] < group_window[:, None, None])
        & (key_pos[None, None, :] >= 0)
    )
    scores = (
        jnp.einsum("qhd,khd->hqk", query_heads, key_heads, preferred_element_type=jnp.float32)
        * score_scale
    )
    masked = jnp.where(allowed, scores, -1e30)
    row_max = jnp.max(masked, axis=-1, keepdims=True)
    weights = jnp.where(allowed, jnp.exp(masked - row_max), 0.0)
    probs = weights / jnp.sum(weights, axis=-1, keepdims=True)
    probs_b = probs.astype(jnp.bfloat16)
    attended = jnp.einsum(
        "hqk,khd->qhd", probs_b, value_heads, preferred_element_type=jnp.float32
    ).astype(jnp.bfloat16)
    grad_probs = jnp.einsum(
        "qhd,khd->hqk", grad_heads, value_heads, preferred_element_type=jnp.float32
    )
    row_term = jnp.sum(probs * grad_probs, axis=-1, keepdims=True)
    grad_scores = (probs * (grad_probs - row_term) * score_scale).astype(jnp.bfloat16)
    grad_query = jnp.einsum(
        "hqk,khd->qhd", grad_scores, key_heads, preferred_element_type=jnp.float32
    )
    grad_key = jnp.einsum(
        "hqk,qhd->khd", grad_scores, query_heads, preferred_element_type=jnp.float32
    )
    grad_value = jnp.einsum("hqk,qhd->khd", probs_b, grad_heads, preferred_element_type=jnp.float32)
    return (attended, grad_query, grad_key, grad_value)


def on_device(token_ids, cotangent, table, w_query, w_key, w_value, w_out, window):
    local_ids = token_ids[0]
    grad_out = cotangent[0]
    length = local_ids.shape[0]
    features = table.shape[1]
    tail_rows = min(length, WINDOW)
    reach_devs = -(-WINDOW // length)
    halo_rows = reach_devs * tail_rows
    offset = lax.axis_index("seq") * length
    own_pos = offset + jnp.arange(length, dtype=jnp.int32)
    halo_pos = offset - halo_rows + jnp.arange(halo_rows, dtype=jnp.int32)
    score_scale = HEAD_DIM ** (-0.5)
    embedded = embed_rows(local_ids, table)
    widened, inv_rms, normed = normalize(embedded)
    query = rotate(jnp.dot(normed, w_query, preferred_element_type=jnp.float32), own_pos).astype(
        jnp.bfloat16
    )
    key_own, value_own = keys_values(normed, own_pos, w_key, w_value)
    key_pieces = []
    value_pieces = []
    for hop_index in range(reach_devs):
        far_keys, far_values = shifted((key_own, value_own), "seq", hop_index + 1)
        key_pieces.insert(0, far_keys)
        value_pieces.insert(0, far_values)
    key_halo = jnp.concatenate(key_pieces, axis=0)
    value_halo = jnp.concatenate(value_pieces, axis=0)
    span_rows = halo_rows + length
    key_all = jnp.concatenate([key_halo, key_own], axis=0)
    value_all = jnp.concatenate([value_halo, value_own], axis=0)
    key_pos = jnp.concatenate([halo_pos, own_pos], axis=0)
    query_heads = query.reshape(length, HEADS, HEAD_DIM)
    key_heads = key_all.reshape(span_rows, HEADS, HEAD_DIM)
    value_heads = value_all.reshape(span_rows, HEADS, HEAD_DIM)
    grad_att = ndot(grad_out, w_out).astype(jnp.bfloat16)
    grad_heads = grad_att.reshape(length, HEADS, HEAD_DIM)
    group_size = 4
    attended_parts = []
    query_parts = []
    key_parts = []
    value_parts = []
    for group_index in range(HEADS // group_size):
        lower = group_index * group_size
        upper = lower + group_size
        outputs = head_group(
            query_heads[:, lower:upper],
            key_heads[:, lower:upper],
            value_heads[:, lower:upper],
            grad_heads[:, lower:upper],
            window[lower:upper],
            own_pos,
            key_pos,
            score_scale,
        )
        attended_parts.append(outputs[0])
        query_parts.append(outputs[1])
        key_parts.append(outputs[2])
        value_parts.append(outputs[3])
    attended = jnp.concatenate(attended_parts, axis=1).reshape(length, features)
    grad_query = jnp.concatenate(query_parts, axis=1).reshape(length, features)
    grad_key = jnp.concatenate(key_parts, axis=1).reshape(span_rows, features)
    grad_value = jnp.concatenate(value_parts, axis=1).reshape(span_rows, features)
    tail_keys = grad_key[:halo_rows].reshape(reach_devs, tail_rows, features)
    tail_values = grad_value[:halo_rows].reshape(reach_devs, tail_rows, features)
    back_keys = jnp.zeros((tail_rows, features), jnp.float32)
    back_values = jnp.zeros((tail_rows, features), jnp.float32)
    for hop_index in range(reach_devs):
        got_keys, got_values = shifted(
            (tail_keys[reach_devs - 1 - hop_index], tail_values[reach_devs - 1 - hop_index]),
            "seq",
            -(hop_index + 1),
        )
        back_keys = back_keys + got_keys
        back_values = back_values + got_values
    own_keys = grad_key[halo_rows:]
    own_values = grad_value[halo_rows:]
    own_keys = jnp.concatenate([own_keys[: length - tail_rows], own_keys + back_keys], axis=0)
    own_values = jnp.concatenate(
        [own_values[: length - tail_rows], own_values + back_values], axis=0
    )
    grad_q_lin = unrotate(grad_query, own_pos).astype(jnp.bfloat16)
    grad_k_lin = unrotate(own_keys, own_pos).astype(jnp.bfloat16)
    grad_v_lin = own_values.astype(jnp.bfloat16)
    grad_normed = ndot(grad_q_lin, w_query) + ndot(grad_k_lin, w_key) + ndot(grad_v_lin, w_value)
    scaled = widened * inv_rms
    grad_input = (
        inv_rms * (grad_normed - scaled * jnp.mean(grad_normed * scaled, axis=1, keepdims=True))
    ).astype(jnp.bfloat16)
    term = jnp.concatenate(
        [
            tdot(normed, grad_q_lin),
            tdot(normed, grad_k_lin),
            tdot(normed, grad_v_lin),
            tdot(attended, grad_out),
        ],
        axis=0,
    )
    shares = lax.psum_scatter(term.astype(jnp.bfloat16), "seq", scatter_dimension=0, tiled=True)
    weight_grads = lax.psum(shares, "dp").astype(jnp.float32)
    return (grad_input[None], weight_grads)


def solution(mesh):
    return jax.shard_map(
        on_device,
        mesh=mesh,
        in_specs=(P("dp", "seq"), P("dp", "seq", None), P(), P(), P(), P(), P(), P()),
        out_specs=(P("dp", "seq", None), P("seq", None)),
        check_vma=False,
    )
```

profile of v0, /device:TPU:2, one launch (start us, length us, event | category | flops | bytes accessed | tf_op | source)
XLA Modules:
  0.0 592.0 jit_solution(5560135934124274321)
XLA Ops:
  14.3 5.2 collective-permute-start.6
  19.5 5.9 %collective-permute-start.5 = (bf16[128,768]{1,0:T(8,128)(2,1)}, bf16[128,768]{1,0:T(8,128)(2,1)}, u32[]{:S(2)}, u32[]{:S(2)}) collective-permute-start(bf16[128,768]{1,0:T(8,128)(2,1)} %convolution_convert_fusion.4), channel_id=1, source_target_pairs={{0,3},{1,4},{2,5},{3,6},{4,7},{5,8},{6,9},{7,10},{8,11},{9,12},{10... | collective-permute-start | bytes 589832 | tf_op jit(solution)/shard_map/ppermute | solution.py:15
  44.0 6.0 %collective-permute-done.4 = bf16[128,768]{1,0:T(8,128)(2,1)} collective-permute-done((bf16[128,768]{1,0:T(8,128)(2,1)}, bf16[128,768]{1,0:T(8,128)(2,1)}, u32[]{:S(2)}, u32[]{:S(2)}) %collective-permute-start.4) | collective-permute-done | bytes 196640 | tf_op jit(solution)/shard_map/ppermute | solution.py:15
  50.0 9.0 %collective-permute-start.2 = (bf16[128,768]{0,1:T(8,128)(2,1)}, bf16[128,768]{0,1:T(8,128)(2,1)}, u32[]{:S(2)}, u32[]{:S(2)}) collective-permute-start(bf16[128,768]{0,1:T(8,128)(2,1)} %bitcast.2), channel_id=1, source_target_pairs={{0,2},{1,3},{2,4},{3,5},{4,6},{5,7},{6,8},{7,9},{8,10},{9,11},{10,... | collective-permute-start | bytes 589832 | tf_op jit(solution)/shard_map/ppermute | solution.py:15
  64.2 5.2 collective-permute-start
  76.5 9.6 %collective-permute-done = bf16[128,768]{0,1:T(8,128)(2,1)} collective-permute-done((bf16[128,768]{0,1:T(8,128)(2,1)}, bf16[128,768]{0,1:T(8,128)(2,1)}, u32[]{:S(2)}, u32[]{:S(2)}) %collective-permute-start) | collective-permute-done | bytes 196640 | tf_op jit(solution)/shard_map/ppermute | solution.py:15
  100.7 6.0 %fusion.55 = f32[128,4,64]{0,2,1:T(8,128)} fusion(bf16[640,12,64]{0,2,1:T(8,128)(2,1)} %bitcast.121, f32[4,128,640]{2,1,0:T(8,128)} %fusion.68, f32[4,128,640]{2,1,0:T(8,128)} %copy-done.8, f32[4,128]{1,0:T(4,128)} %copy-done.43), kind=kOutput, calls=%fused_computation.66 | convolution fusion | flops 44237952 | bytes 3737600 | tf_op jit(solution)/shard_map/hqk,khd->qhd/dot_general | solution.py:109
  106.7 6.1 %convolution_bitcast_fusion.3 = f32[640,4,64]{0,2,1:T(8,128)} fusion(f32[4,128,640]{2,1,0:T(8,128)} %fusion.68, bf16[128,12,32]{0,2,1:T(8,128)(2,1)} %get-tuple-element.17, bf16[128,12,32]{0,2,1:T(8,128)(2,1)} %get-tuple-element.16, f32[4,128,640]{2,1,0:T(8,128)} %copy-done.8, f32[4,128]{1,0:T(4,128)} %copy-done.43), kind=kOutput, calls=%fused_computation.46 | convolution fusion | flops 44631168 | bytes 3475456 | tf_op jit(solution)/shard_map/hqk,qhd->khd/dot_general | solution.py:112
  119.8 5.8 fusion.52
  125.6 6.0 %convolution_bitcast_fusion.4 = f32[640,4,64]{0,2,1:T(8,128)} fusion(f32[4,128,640]{2,1,0:T(8,128)} %fusion.71, bf16[128,12,32]{0,2,1:T(8,128)(2,1)} %get-tuple-element.17, bf16[128,12,32]{0,2,1:T(8,128)(2,1)} %get-tuple-element.16, f32[4,128,640]{2,1,0:T(8,128)} %copy-done.9, f32[4,128]{1,0:T(4,128)} %copy-done.44), kind=kOutput, calls=%fused_computation.47 | convolution fusion | flops 44631168 | bytes 3475456 | tf_op jit(solution)/shard_map/hqk,qhd->khd/dot_general | solution.py:112
  138.0 5.2 fusion.49
  143.2 5.9 convolution_bitcast_fusion.5
  156.7 4.5 collective-permute-start.13
  167.6 10.3 %collective-permute-done.15 = f32[128,768]{0,1:T(8,128)S(1)} collective-permute-done((f32[128,768]{0,1:T(8,128)S(1)}, f32[128,768]{0,1:T(8,128)S(1)}, u32[]{:S(2)}, u32[]{:S(2)}) %collective-permute-start.15) | collective-permute-done | bytes 393248 | tf_op jit(solution)/shard_map/ppermute | solution.py:15
  177.9 7.2 %collective-permute-start.9 = (f32[128,768]{0,1:T(8,128)S(1)}, f32[128,768]{0,1:T(8,128)S(1)}, u32[]{:S(2)}, u32[]{:S(2)}) collective-permute-start(f32[128,768]{0,1:T(8,128)S(1)} %bitcast.114), channel_id=1, source_target_pairs={{2,0},{3,1},{4,2},{5,3},{6,4},{7,5},{8,6},{9,7},{10,8},{11,9},{12,... | collective-permute-start | bytes 1179656 | tf_op jit(solution)/shard_map/ppermute | solution.py:15
  185.1 13.0 %collective-permute-done.13 = f32[128,768]{0,1:T(8,128)S(1)} collective-permute-done((f32[128,768]{0,1:T(8,128)S(1)}, f32[128,768]{0,1:T(8,128)S(1)}, u32[]{:S(2)}, u32[]{:S(2)}) %collective-permute-start.13) | collective-permute-done | bytes 393248 | tf_op jit(solution)/shard_map/ppermute | solution.py:15
  198.1 10.3 %collective-permute-start.10 = (f32[128,768]{0,1:T(8,128)S(1)}, f32[128,768]{0,1:T(8,128)S(1)}, u32[]{:S(2)}, u32[]{:S(2)}) collective-permute-start(f32[128,768]{0,1:T(8,128)S(1)} %bitcast.113), channel_id=1, source_target_pairs={{3,0},{4,1},{5,2},{6,3},{7,4},{8,5},{9,6},{10,7},{11,8},{12,9},{13... | collective-permute-start | bytes 1179656 | tf_op jit(solution)/shard_map/ppermute | solution.py:15
  208.4 9.7 %collective-permute-done.14 = f32[128,768]{0,1:T(8,128)S(1)} collective-permute-done((f32[128,768]{0,1:T(8,128)S(1)}, f32[128,768]{0,1:T(8,128)S(1)}, u32[]{:S(2)}, u32[]{:S(2)}) %collective-permute-start.14) | collective-permute-done | bytes 393248 | tf_op jit(solution)/shard_map/ppermute | solution.py:15
  220.0 28.5 %collective-permute-done.12 = f32[128,768]{0,1:T(8,128)S(1)} collective-permute-done((f32[128,768]{0,1:T(8,128)S(1)}, f32[128,768]{0,1:T(8,128)S(1)}, u32[]{:S(2)}, u32[]{:S(2)}) %collective-permute-start.12) | collective-permute-done | bytes 393248 | tf_op jit(solution)/shard_map/ppermute | solution.py:15
  249.3 17.1 %collective-permute-done.9 = f32[128,768]{0,1:T(8,128)S(1)} collective-permute-done((f32[128,768]{0,1:T(8,128)S(1)}, f32[128,768]{0,1:T(8,128)S(1)}, u32[]{:S(2)}, u32[]{:S(2)}) %collective-permute-start.9) | collective-permute-done | bytes 393248 | tf_op jit(solution)/shard_map/ppermute | solution.py:15
  266.3 18.8 %collective-permute-done.10 = f32[128,768]{0,1:T(8,128)S(1)} collective-permute-done((f32[128,768]{0,1:T(8,128)S(1)}, f32[128,768]{0,1:T(8,128)S(1)}, u32[]{:S(2)}, u32[]{:S(2)}) %collective-permute-start.10) | collective-permute-done | bytes 393248 | tf_op jit(solution)/shard_map/ppermute | solution.py:15
  285.1 8.3 %collective-permute-done.8 = f32[128,768]{0,1:T(8,128)S(1)} collective-permute-done((f32[128,768]{0,1:T(8,128)S(1)}, f32[128,768]{0,1:T(8,128)S(1)}, u32[]{:S(2)}, u32[]{:S(2)}) %collective-permute-start.8) | collective-permute-done | bytes 393248 | tf_op jit(solution)/shard_map/ppermute | solution.py:15
  300.0 219.1 %reduce-scatter.2.cloned.1.call-done = bf16[96,768]{1,0:T(8,128)(2,1)} async-done(((bf16[3072,768]{1,0:T(8,128)(2,1)}), bf16[96,768]{1,0:T(8,128)(2,1)}) %reduce-scatter.2.cloned.1.call-update) | async-done | bytes 147472 | tf_op jit(solution)/shard_map/reduce_scatter | solution.py:215
  519.9 63.7 %all-reduce.2.cloned.1.call-done = bf16[96,768]{1,0:T(8,128)(2,1)} async-done(((bf16[96,768]{1,0:T(8,128)(2,1)}), bf16[96,768]{1,0:T(8,128)(2,1)}) %all-reduce.2.cloned.1.call-update) | async-done | bytes 147472 | tf_op jit(solution)/shard_map/psum | solution.py:216
  (183 shorter events, 90.6 us)
Async XLA Ops:
  7.2 511.9 %reduce-scatter.2.cloned.1.call-start = ((), (), s32[]{:S(2)}) async-start(), calls=%async_computation.1 | async-start | bytes 4866048 | tf_op jit(solution)/shard_map/reduce_scatter | solution.py:215
  7.2 21.6 %copy-start.1 = (bf16[768,768]{1,0:T(8,128)(2,1)S(1)}, bf16[768,768]{1,0:T(8,128)(2,1)}, u32[]{:S(2)}) copy-start(bf16[768,768]{1,0:T(8,128)(2,1)} %param.11) | copy-start | bytes 3538948
  10.5 60.5 %collective-permute-start.7 = (bf16[128,768]{1,0:T(8,128)(2,1)}, bf16[128,768]{1,0:T(8,128)(2,1)}, u32[]{:S(2)}, u32[]{:S(2)}) collective-permute-start(bf16[128,768]{1,0:T(8,128)(2,1)} %convolution_convert_fusion.4), channel_id=1, source_target_pairs={{0,1},{1,2},{2,3},{3,4},{4,5},{5,6},{6,7},{7,8},{8,9},{9,10},{10,1... | collective-permute-start | bytes 589832 | tf_op jit(solution)/shard_map/ppermute | solution.py:15
  14.3 49.9 %collective-permute-start.6 = (bf16[128,768]{1,0:T(8,128)(2,1)}, bf16[128,768]{1,0:T(8,128)(2,1)}, u32[]{:S(2)}, u32[]{:S(2)}) collective-permute-start(bf16[128,768]{1,0:T(8,128)(2,1)} %convolution_convert_fusion.4), channel_id=1, source_target_pairs={{0,2},{1,3},{2,4},{3,5},{4,6},{5,7},{6,8},{7,9},{8,10},{9,11},{10,... | collective-permute-start | bytes 589832 | tf_op jit(solution)/shard_map/ppermute | solution.py:15
  19.5 41.1 %collective-permute-start.5 = (bf16[128,768]{1,0:T(8,128)(2,1)}, bf16[128,768]{1,0:T(8,128)(2,1)}, u32[]{:S(2)}, u32[]{:S(2)}) collective-permute-start(bf16[128,768]{1,0:T(8,128)(2,1)} %convolution_convert_fusion.4), channel_id=1, source_target_pairs={{0,3},{1,4},{2,5},{3,6},{4,7},{5,8},{6,9},{7,10},{8,11},{9,12},{10... | collective-permute-start | bytes 589832 | tf_op jit(solution)/shard_map/ppermute | solution.py:15
  25.4 24.5 %collective-permute-start.4 = (bf16[128,768]{1,0:T(8,128)(2,1)}, bf16[128,768]{1,0:T(8,128)(2,1)}, u32[]{:S(2)}, u32[]{:S(2)}) collective-permute-start(bf16[128,768]{1,0:T(8,128)(2,1)} %convolution_convert_fusion.4), channel_id=1, source_target_pairs={{0,4},{1,5},{2,6},{3,7},{4,8},{5,9},{6,10},{7,11},{8,12},{9,13},{1... | collective-permute-start | bytes 589832 | tf_op jit(solution)/shard_map/ppermute | solution.py:15
  32.4 62.0 %collective-permute-start.3 = (bf16[128,768]{0,1:T(8,128)(2,1)}, bf16[128,768]{0,1:T(8,128)(2,1)}, u32[]{:S(2)}, u32[]{:S(2)}) collective-permute-start(bf16[128,768]{0,1:T(8,128)(2,1)} %bitcast.2), channel_id=1, source_target_pairs={{0,1},{1,2},{2,3},{3,4},{4,5},{5,6},{6,7},{7,8},{8,9},{9,10},{10,1... | collective-permute-start | bytes 589832 | tf_op jit(solution)/shard_map/ppermute | solution.py:15
  50.0 42.0 %collective-permute-start.2 = (bf16[128,768]{0,1:T(8,128)(2,1)}, bf16[128,768]{0,1:T(8,128)(2,1)}, u32[]{:S(2)}, u32[]{:S(2)}) collective-permute-start(bf16[128,768]{0,1:T(8,128)(2,1)} %bitcast.2), channel_id=1, source_target_pairs={{0,2},{1,3},{2,4},{3,5},{4,6},{5,7},{6,8},{7,9},{8,10},{9,11},{10,... | collective-permute-start | bytes 589832 | tf_op jit(solution)/shard_map/ppermute | solution.py:15
  60.6 28.8 %collective-permute-start.1 = (bf16[128,768]{0,1:T(8,128)(2,1)}, bf16[128,768]{0,1:T(8,128)(2,1)}, u32[]{:S(2)}, u32[]{:S(2)}) collective-permute-start(bf16[128,768]{0,1:T(8,128)(2,1)} %bitcast.2), channel_id=1, source_target_pairs={{0,3},{1,4},{2,5},{3,6},{4,7},{5,8},{6,9},{7,10},{8,11},{9,12},{10... | collective-permute-start | bytes 589832 | tf_op jit(solution)/shard_map/ppermute | solution.py:15
  64.2 21.9 %collective-permute-start = (bf16[128,768]{0,1:T(8,128)(2,1)}, bf16[128,768]{0,1:T(8,128)(2,1)}, u32[]{:S(2)}, u32[]{:S(2)}) collective-permute-start(bf16[128,768]{0,1:T(8,128)(2,1)} %bitcast.2), channel_id=1, source_target_pairs={{0,4},{1,5},{2,6},{3,7},{4,8},{5,9},{6,10},{7,11},{8,12},{9,13},{1... | collective-permute-start | bytes 589832 | tf_op jit(solution)/shard_map/ppermute | solution.py:15
  152.8 14.2 %copy-start.31 = (bf16[128,4,64]{0,2,1:T(8,128)(2,1)S(1)}, bf16[128,4,64]{0,2,1:T(8,128)(2,1)}, u32[]{:S(2)}) copy-start(bf16[128,4,64]{0,2,1:T(8,128)(2,1)} %fusion.60) | copy-start | bytes 196612
  152.8 14.2 %copy-start.21 = (f32[128,4,64]{0,2,1:T(8,128)S(1)}, f32[128,4,64]{0,2,1:T(8,128)}, u32[]{:S(2)}) copy-start(f32[128,4,64]{0,2,1:T(8,128)} %fusion.55) | copy-start | bytes 393220
  152.8 14.2 %copy-start.22 = (f32[128,4,64]{0,2,1:T(8,128)S(1)}, f32[128,4,64]{0,2,1:T(8,128)}, u32[]{:S(2)}) copy-start(f32[128,4,64]{0,2,1:T(8,128)} %fusion.52) | copy-start | bytes 393220
  153.1 24.8 %collective-permute-start.15 = (f32[128,768]{0,1:T(8,128)S(1)}, f32[128,768]{0,1:T(8,128)S(1)}, u32[]{:S(2)}, u32[]{:S(2)}) collective-permute-start(f32[128,768]{0,1:T(8,128)S(1)} %bitcast.119), channel_id=1, source_target_pairs={{4,0},{5,1},{6,2},{7,3},{8,4},{9,5},{10,6},{11,7},{12,8},{13,9},{1... | collective-permute-start | bytes 1179656 | tf_op jit(solution)/shard_map/ppermute | solution.py:15
  156.7 41.5 %collective-permute-start.13 = (f32[128,768]{0,1:T(8,128)S(1)}, f32[128,768]{0,1:T(8,128)S(1)}, u32[]{:S(2)}, u32[]{:S(2)}) collective-permute-start(f32[128,768]{0,1:T(8,128)S(1)} %bitcast.118), channel_id=1, source_target_pairs={{2,0},{3,1},{4,2},{5,3},{6,4},{7,5},{8,6},{9,7},{10,8},{11,9},{12,... | collective-permute-start | bytes 1179656 | tf_op jit(solution)/shard_map/ppermute | solution.py:15
  161.2 56.9 %collective-permute-start.14 = (f32[128,768]{0,1:T(8,128)S(1)}, f32[128,768]{0,1:T(8,128)S(1)}, u32[]{:S(2)}, u32[]{:S(2)}) collective-permute-start(f32[128,768]{0,1:T(8,128)S(1)} %bitcast.117), channel_id=1, source_target_pairs={{3,0},{4,1},{5,2},{6,3},{7,4},{8,5},{9,6},{10,7},{11,8},{12,9},{13... | collective-permute-start | bytes 1179656 | tf_op jit(solution)/shard_map/ppermute | solution.py:15
  163.1 85.5 %collective-permute-start.12 = (f32[128,768]{0,1:T(8,128)S(1)}, f32[128,768]{0,1:T(8,128)S(1)}, u32[]{:S(2)}, u32[]{:S(2)}) collective-permute-start(f32[128,768]{0,1:T(8,128)S(1)} %bitcast.116), channel_id=1, source_target_pairs={{1,0},{2,1},{3,2},{4,3},{5,4},{6,5},{7,6},{8,7},{9,8},{10,9},{11,1... | collective-permute-start | bytes 1179656 | tf_op jit(solution)/shard_map/ppermute | solution.py:15
  165.1 84.2 %collective-permute-start.11 = (f32[128,768]{0,1:T(8,128)S(1)}, f32[128,768]{0,1:T(8,128)S(1)}, u32[]{:S(2)}, u32[]{:S(2)}) collective-permute-start(f32[128,768]{0,1:T(8,128)S(1)} %bitcast.115), channel_id=1, source_target_pairs={{4,0},{5,1},{6,2},{7,3},{8,4},{9,5},{10,6},{11,7},{12,8},{13,9},{1... | collective-permute-start | bytes 1179656 | tf_op jit(solution)/shard_map/ppermute | solution.py:15
  177.9 88.5 %collective-permute-start.9 = (f32[128,768]{0,1:T(8,128)S(1)}, f32[128,768]{0,1:T(8,128)S(1)}, u32[]{:S(2)}, u32[]{:S(2)}) collective-permute-start(f32[128,768]{0,1:T(8,128)S(1)} %bitcast.114), channel_id=1, source_target_pairs={{2,0},{3,1},{4,2},{5,3},{6,4},{7,5},{8,6},{9,7},{10,8},{11,9},{12,... | collective-permute-start | bytes 1179656 | tf_op jit(solution)/shard_map/ppermute | solution.py:15
  198.1 87.0 %collective-permute-start.10 = (f32[128,768]{0,1:T(8,128)S(1)}, f32[128,768]{0,1:T(8,128)S(1)}, u32[]{:S(2)}, u32[]{:S(2)}) collective-permute-start(f32[128,768]{0,1:T(8,128)S(1)} %bitcast.113), channel_id=1, source_target_pairs={{3,0},{4,1},{5,2},{6,3},{7,4},{8,5},{9,6},{10,7},{11,8},{12,9},{13... | collective-permute-start | bytes 1179656 | tf_op jit(solution)/shard_map/ppermute | solution.py:15
  218.1 75.3 %collective-permute-start.8 = (f32[128,768]{0,1:T(8,128)S(1)}, f32[128,768]{0,1:T(8,128)S(1)}, u32[]{:S(2)}, u32[]{:S(2)}) collective-permute-start(f32[128,768]{0,1:T(8,128)S(1)} %bitcast.112), channel_id=1, source_target_pairs={{1,0},{2,1},{3,2},{4,3},{5,4},{6,5},{7,6},{8,7},{9,8},{10,9},{11,1... | collective-permute-start | bytes 1179656 | tf_op jit(solution)/shard_map/ppermute | solution.py:15
  249.2 44.4 %copy-start.18 = (f32[128,32]{0,1:T(8,128)S(1)}, f32[128,32]{0,1:T(8,128)}, u32[]{:S(2)}) copy-start(f32[128,32]{0,1:T(8,128)} %copy-done.17) | copy-start | bytes 49156
  249.2 44.4 %copy-start.20 = (f32[128,32]{0,1:T(8,128)S(1)}, f32[128,32]{0,1:T(8,128)}, u32[]{:S(2)}) copy-start(f32[128,32]{0,1:T(8,128)} %copy-done.19) | copy-start | bytes 49156
  297.3 286.2 %all-reduce.2.cloned.1.call-start = ((), (), s32[]{:S(2)}) async-start(), calls=%async_computation.2 | async-start | bytes 294912 | tf_op jit(solution)/shard_map/psum | solution.py:216
  (42 other events, 132.4 us)
Sparse Core Ops, SparseCore 0:
  297.5 221.5 reduce-scatter.1
  521.4 62.1 all-reduce.1
where the time goes:
time: 593 us; the launch traced here: 592 us
  waiting for transfers between devices  404 us (68%)
  starting transfers between devices  71.6 us (12%)
  matrix products  63.4 us (11%)
  local copies, waits for them, and re-layouts  26.3 us (4%)
  between operations  14.9 us (3%)
  other arithmetic  11.7 us (2%)
    reduce_scatter x1, waiting for transfers between devices, on_device(): lax.psum_scatter(term.astype(jnp.bfloat16), 'seq', scatter_dimension=0, t...  219 us
    ppermute x16, waiting for transfers between devices, shifted(): return lax.ppermute(block, axis, route)  121 us
    ppermute x16, starting transfers between devices, shifted(): return lax.ppermute(block, axis, route)  71.5 us
    psum x1, waiting for transfers between devices, on_device(): weight_grads = lax.psum(shares, 'dp').astype(jnp.float32)  63.7 us
    unnamed x104, local copies, waits for them, and re-layouts  18.4 us
    dot_general x3, matrix products, head_group(): jnp.einsum('hqk,qhd->khd', grad_scores, query_heads, preferred_element_ty...  18.1 us
    dot_general x3, matrix products, head_group(): jnp.einsum('hqk,khd->qhd', grad_scores, key_heads, preferred_element_type...  17 us
  transfers between devices with their start and end apart: 18, of which 11 were waited for; matrix products, arithmetic and copies ran while one was open for 5% of the time, Pallas kernels for 0%

commit v1 on v0

--- a/solution.py
+++ b/solution.py
@@ -213,7 +213,11 @@
         axis=0,
     )
     shares = lax.psum_scatter(term.astype(jnp.bfloat16), "seq", scatter_dimension=0, tiled=True)
-    weight_grads = lax.psum(shares, "dp").astype(jnp.float32)
+
+    def put_levels_all(shard_in):
+        return lax.all_gather(shard_in, "dp").sum(axis=0)
+
+    weight_grads = put_levels_all(shares).astype(jnp.float32)
     return (grad_input[None], weight_grads)
 
 

time: 593 us -> 558 us (0.941)
  waiting for transfers between devices: 404 us -> 367 us
    psum x1 -> x0, waiting for transfers between devices: 63.7 us -> none  [on_device(): weight_grads = lax.psum(shares, 'dp').astype(jnp.float32)]
    all_gather x0 -> x1, waiting for transfers between devices: none -> 23.9 us  [put_levels_all(): return lax.all_gather(shard_in, 'dp').sum(axis=0)]
  transfers between devices with their start and end apart: 18 -> 18, of which waited for: 11 -> 11; matrix products, arithmetic and copies ran while one was open for 5% -> 6% of each run, Pallas kernels for 0% -> 0%
where the time goes in v1:
time: 558 us; the launch traced here: 555 us
  waiting for transfers between devices  367 us (66%)
  starting transfers between devices  71.6 us (13%)
  matrix products  63.4 us (11%)
  local copies, waits for them, and re-layouts  26.3 us (5%)
  between operations  14.9 us (3%)
  other arithmetic  12.2 us (2%)
    reduce_scatter x1, waiting for transfers between devices, on_device(): lax.psum_scatter(term.astype(jnp.bfloat16), 'seq', scatter_dimension=0, t...  222 us
    ppermute x16, waiting for transfers between devices, shifted(): return lax.ppermute(block, axis, route)  121 us
    ppermute x16, starting transfers between devices, shifted(): return lax.ppermute(block, axis, route)  71.5 us
    all_gather x1, waiting for transfers between devices, put_levels_all(): return lax.all_gather(shard_in, 'dp').sum(axis=0)  23.9 us
    unnamed x104, local copies, waits for them, and re-layouts  18.4 us
    dot_general x3, matrix products, head_group(): jnp.einsum('hqk,qhd->khd', grad_scores, query_heads, preferred_element_ty...  18.1 us
    dot_general x3, matrix products, head_group(): jnp.einsum('hqk,khd->qhd', grad_scores, key_heads, preferred_element_type...  17 us
  transfers between devices with their start and end apart: 18, of which 11 were waited for; matrix products, arithmetic and copies ran while one was open for 6% of the time, Pallas kernels for 0%

profile of v1, /device:TPU:2, one launch (start us, length us, event | category | flops | bytes accessed | tf_op | source)
XLA Modules:
  0.0 555.4 jit_solution(18248105114631787160)
XLA Ops:
  14.3 5.2 collective-permute-start.6
  19.5 5.9 %collective-permute-start.5 = (bf16[128,768]{1,0:T(8,128)(2,1)}, bf16[128,768]{1,0:T(8,128)(2,1)}, u32[]{:S(2)}, u32[]{:S(2)}) collective-permute-start(bf16[128,768]{1,0:T(8,128)(2,1)} %convolution_convert_fusion.4), channel_id=1, source_target_pairs={{0,3},{1,4},{2,5},{3,6},{4,7},{5,8},{6,9},{7,10},{8,11},{9,12},{10... | collective-permute-start | bytes 589832 | tf_op jit(solution)/shard_map/ppermute | solution.py:15
  44.0 6.0 %collective-permute-done.4 = bf16[128,768]{1,0:T(8,128)(2,1)} collective-permute-done((bf16[128,768]{1,0:T(8,128)(2,1)}, bf16[128,768]{1,0:T(8,128)(2,1)}, u32[]{:S(2)}, u32[]{:S(2)}) %collective-permute-start.4) | collective-permute-done | bytes 196640 | tf_op jit(solution)/shard_map/ppermute | solution.py:15
  50.0 9.0 %collective-permute-start.2 = (bf16[128,768]{0,1:T(8,128)(2,1)}, bf16[128,768]{0,1:T(8,128)(2,1)}, u32[]{:S(2)}, u32[]{:S(2)}) collective-permute-start(bf16[128,768]{0,1:T(8,128)(2,1)} %bitcast.2), channel_id=1, source_target_pairs={{0,2},{1,3},{2,4},{3,5},{4,6},{5,7},{6,8},{7,9},{8,10},{9,11},{10,... | collective-permute-start | bytes 589832 | tf_op jit(solution)/shard_map/ppermute | solution.py:15
  64.2 5.2 collective-permute-start
  76.5 9.6 %collective-permute-done = bf16[128,768]{0,1:T(8,128)(2,1)} collective-permute-done((bf16[128,768]{0,1:T(8,128)(2,1)}, bf16[128,768]{0,1:T(8,128)(2,1)}, u32[]{:S(2)}, u32[]{:S(2)}) %collective-permute-start) | collective-permute-done | bytes 196640 | tf_op jit(solution)/shard_map/ppermute | solution.py:15
  100.7 6.0 %fusion.55 = f32[128,4,64]{0,2,1:T(8,128)} fusion(bf16[640,12,64]{0,2,1:T(8,128)(2,1)} %bitcast.123, f32[4,128,640]{2,1,0:T(8,128)} %fusion.68, f32[4,128,640]{2,1,0:T(8,128)} %copy-done.8, f32[4,128]{1,0:T(4,128)} %copy-done.43), kind=kOutput, calls=%fused_computation.66 | convolution fusion | flops 44237952 | bytes 3737600 | tf_op jit(solution)/shard_map/hqk,khd->qhd/dot_general | solution.py:109
  106.7 6.1 %convolution_bitcast_fusion.3 = f32[640,4,64]{0,2,1:T(8,128)} fusion(f32[4,128,640]{2,1,0:T(8,128)} %fusion.68, bf16[128,12,32]{0,2,1:T(8,128)(2,1)} %get-tuple-element.17, bf16[128,12,32]{0,2,1:T(8,128)(2,1)} %get-tuple-element.16, f32[4,128,640]{2,1,0:T(8,128)} %copy-done.8, f32[4,128]{1,0:T(4,128)} %copy-done.43), kind=kOutput, calls=%fused_computation.46 | convolution fusion | flops 44631168 | bytes 3475456 | tf_op jit(solution)/shard_map/hqk,qhd->khd/dot_general | solution.py:112
  119.8 5.8 %fusion.52 = f32[128,4,64]{0,2,1:T(8,128)} fusion(bf16[640,12,64]{0,2,1:T(8,128)(2,1)} %bitcast.125, f32[4,128,640]{2,1,0:T(8,128)} %fusion.71, f32[4,128,640]{2,1,0:T(8,128)} %copy-done.9, f32[4,128]{1,0:T(4,128)} %copy-done.44), kind=kOutput, calls=%fused_computation.65 | convolution fusion | flops 44237952 | bytes 3737600 | tf_op jit(solution)/shard_map/hqk,khd->qhd/dot_general | solution.py:109
  125.6 6.0 %convolution_bitcast_fusion.4 = f32[640,4,64]{0,2,1:T(8,128)} fusion(f32[4,128,640]{2,1,0:T(8,128)} %fusion.71, bf16[128,12,32]{0,2,1:T(8,128)(2,1)} %get-tuple-element.17, bf16[128,12,32]{0,2,1:T(8,128)(2,1)} %get-tuple-element.16, f32[4,128,640]{2,1,0:T(8,128)} %copy-done.9, f32[4,128]{1,0:T(4,128)} %copy-done.44), kind=kOutput, calls=%fused_computation.47 | convolution fusion | flops 44631168 | bytes 3475456 | tf_op jit(solution)/shard_map/hqk,qhd->khd/dot_general | solution.py:112
  138.0 5.2 fusion.49
  143.2 5.9 %convolution_bitcast_fusion.5 = f32[640,4,64]{0,2,1:T(8,128)} fusion(f32[4,128,640]{2,1,0:T(8,128)} %fusion.74, bf16[128,12,32]{0,2,1:T(8,128)(2,1)S(1)} %copy-done.30, bf16[128,12,32]{0,2,1:T(8,128)(2,1)S(1)} %copy-done.26, f32[4,128,640]{2,1,0:T(8,128)} %copy-done.7, f32[4,128]{1,0:T(4,128)S(1)} %copy-done.42), kind=kOutput, calls=%fused_computation.48 | convolution fusion | flops 44631168 | bytes 3475456 | tf_op jit(solution)/shard_map/hqk,qhd->khd/dot_general | solution.py:112
  156.7 4.5 collective-permute-start.13
  167.6 10.3 %collective-permute-done.15 = f32[128,768]{0,1:T(8,128)S(1)} collective-permute-done((f32[128,768]{0,1:T(8,128)S(1)}, f32[128,768]{0,1:T(8,128)S(1)}, u32[]{:S(2)}, u32[]{:S(2)}) %collective-permute-start.15) | collective-permute-done | bytes 393248 | tf_op jit(solution)/shard_map/ppermute | solution.py:15
  177.9 7.2 %collective-permute-start.9 = (f32[128,768]{0,1:T(8,128)S(1)}, f32[128,768]{0,1:T(8,128)S(1)}, u32[]{:S(2)}, u32[]{:S(2)}) collective-permute-start(f32[128,768]{0,1:T(8,128)S(1)} %bitcast.116), channel_id=1, source_target_pairs={{2,0},{3,1},{4,2},{5,3},{6,4},{7,5},{8,6},{9,7},{10,8},{11,9},{12,... | collective-permute-start | bytes 1179656 | tf_op jit(solution)/shard_map/ppermute | solution.py:15
  185.1 13.0 %collective-permute-done.13 = f32[128,768]{0,1:T(8,128)S(1)} collective-permute-done((f32[128,768]{0,1:T(8,128)S(1)}, f32[128,768]{0,1:T(8,128)S(1)}, u32[]{:S(2)}, u32[]{:S(2)}) %collective-permute-start.13) | collective-permute-done | bytes 393248 | tf_op jit(solution)/shard_map/ppermute | solution.py:15
  198.1 10.3 %collective-permute-start.10 = (f32[128,768]{0,1:T(8,128)S(1)}, f32[128,768]{0,1:T(8,128)S(1)}, u32[]{:S(2)}, u32[]{:S(2)}) collective-permute-start(f32[128,768]{0,1:T(8,128)S(1)} %bitcast.115), channel_id=1, source_target_pairs={{3,0},{4,1},{5,2},{6,3},{7,4},{8,5},{9,6},{10,7},{11,8},{12,9},{13... | collective-permute-start | bytes 1179656 | tf_op jit(solution)/shard_map/ppermute | solution.py:15
  208.4 9.7 %collective-permute-done.14 = f32[128,768]{0,1:T(8,128)S(1)} collective-permute-done((f32[128,768]{0,1:T(8,128)S(1)}, f32[128,768]{0,1:T(8,128)S(1)}, u32[]{:S(2)}, u32[]{:S(2)}) %collective-permute-start.14) | collective-permute-done | bytes 393248 | tf_op jit(solution)/shard_map/ppermute | solution.py:15
  220.0 28.5 %collective-permute-done.12 = f32[128,768]{0,1:T(8,128)S(1)} collective-permute-done((f32[128,768]{0,1:T(8,128)S(1)}, f32[128,768]{0,1:T(8,128)S(1)}, u32[]{:S(2)}, u32[]{:S(2)}) %collective-permute-start.12) | collective-permute-done | bytes 393248 | tf_op jit(solution)/shard_map/ppermute | solution.py:15
  249.3 17.1 %collective-permute-done.9 = f32[128,768]{0,1:T(8,128)S(1)} collective-permute-done((f32[128,768]{0,1:T(8,128)S(1)}, f32[128,768]{0,1:T(8,128)S(1)}, u32[]{:S(2)}, u32[]{:S(2)}) %collective-permute-start.9) | collective-permute-done | bytes 393248 | tf_op jit(solution)/shard_map/ppermute | solution.py:15
  266.3 18.8 %collective-permute-done.10 = f32[128,768]{0,1:T(8,128)S(1)} collective-permute-done((f32[128,768]{0,1:T(8,128)S(1)}, f32[128,768]{0,1:T(8,128)S(1)}, u32[]{:S(2)}, u32[]{:S(2)}) %collective-permute-start.10) | collective-permute-done | bytes 393248 | tf_op jit(solution)/shard_map/ppermute | solution.py:15
  285.1 8.3 %collective-permute-done.8 = f32[128,768]{0,1:T(8,128)S(1)} collective-permute-done((f32[128,768]{0,1:T(8,128)S(1)}, f32[128,768]{0,1:T(8,128)S(1)}, u32[]{:S(2)}, u32[]{:S(2)}) %collective-permute-start.8) | collective-permute-done | bytes 393248 | tf_op jit(solution)/shard_map/ppermute | solution.py:15
  297.4 221.7 %reduce-scatter.2.cloned.1.call-done = bf16[96,768]{1,0:T(8,128)(2,1)} async-done(((bf16[3072,768]{1,0:T(8,128)(2,1)}), bf16[96,768]{1,0:T(8,128)(2,1)}) %reduce-scatter.2.cloned.1.call-update) | async-done | bytes 147472 | tf_op jit(solution)/shard_map/reduce_scatter | solution.py:215
  522.5 23.9 %all-gather.3.cloned.1.call-done = bf16[768,768]{1,0:T(8,128)(2,1)} async-done(((bf16[96,768]{1,0:T(8,128)(2,1)}), bf16[768,768]{1,0:T(8,128)(2,1)}) %all-gather.3.cloned.1.call-update) | async-done | bytes 1179664 | tf_op jit(solution)/shard_map/all_gather | solution.py:218
  (184 shorter events, 91.1 us)
Async XLA Ops:
  7.2 511.9 %reduce-scatter.2.cloned.1.call-start = ((), (), s32[]{:S(2)}) async-start(), calls=%async_computation.1 | async-start | bytes 4866048 | tf_op jit(solution)/shard_map/reduce_scatter | solution.py:215
  7.2 21.6 %copy-start.1 = (bf16[768,768]{1,0:T(8,128)(2,1)S(1)}, bf16[768,768]{1,0:T(8,128)(2,1)}, u32[]{:S(2)}) copy-start(bf16[768,768]{1,0:T(8,128)(2,1)} %param.11) | copy-start | bytes 3538948
  10.5 60.5 %collective-permute-start.7 = (bf16[128,768]{1,0:T(8,128)(2,1)}, bf16[128,768]{1,0:T(8,128)(2,1)}, u32[]{:S(2)}, u32[]{:S(2)}) collective-permute-start(bf16[128,768]{1,0:T(8,128)(2,1)} %convolution_convert_fusion.4), channel_id=1, source_target_pairs={{0,1},{1,2},{2,3},{3,4},{4,5},{5,6},{6,7},{7,8},{8,9},{9,10},{10,1... | collective-permute-start | bytes 589832 | tf_op jit(solution)/shard_map/ppermute | solution.py:15
  14.3 49.9 %collective-permute-start.6 = (bf16[128,768]{1,0:T(8,128)(2,1)}, bf16[128,768]{1,0:T(8,128)(2,1)}, u32[]{:S(2)}, u32[]{:S(2)}) collective-permute-start(bf16[128,768]{1,0:T(8,128)(2,1)} %convolution_convert_fusion.4), channel_id=1, source_target_pairs={{0,2},{1,3},{2,4},{3,5},{4,6},{5,7},{6,8},{7,9},{8,10},{9,11},{10,... | collective-permute-start | bytes 589832 | tf_op jit(solution)/shard_map/ppermute | solution.py:15
  19.5 41.1 %collective-permute-start.5 = (bf16[128,768]{1,0:T(8,128)(2,1)}, bf16[128,768]{1,0:T(8,128)(2,1)}, u32[]{:S(2)}, u32[]{:S(2)}) collective-permute-start(bf16[128,768]{1,0:T(8,128)(2,1)} %convolution_convert_fusion.4), channel_id=1, source_target_pairs={{0,3},{1,4},{2,5},{3,6},{4,7},{5,8},{6,9},{7,10},{8,11},{9,12},{10... | collective-permute-start | bytes 589832 | tf_op jit(solution)/shard_map/ppermute | solution.py:15
  25.4 24.5 %collective-permute-start.4 = (bf16[128,768]{1,0:T(8,128)(2,1)}, bf16[128,768]{1,0:T(8,128)(2,1)}, u32[]{:S(2)}, u32[]{:S(2)}) collective-permute-start(bf16[128,768]{1,0:T(8,128)(2,1)} %convolution_convert_fusion.4), channel_id=1, source_target_pairs={{0,4},{1,5},{2,6},{3,7},{4,8},{5,9},{6,10},{7,11},{8,12},{9,13},{1... | collective-permute-start | bytes 589832 | tf_op jit(solution)/shard_map/ppermute | solution.py:15
  32.4 62.0 %collective-permute-start.3 = (bf16[128,768]{0,1:T(8,128)(2,1)}, bf16[128,768]{0,1:T(8,128)(2,1)}, u32[]{:S(2)}, u32[]{:S(2)}) collective-permute-start(bf16[128,768]{0,1:T(8,128)(2,1)} %bitcast.2), channel_id=1, source_target_pairs={{0,1},{1,2},{2,3},{3,4},{4,5},{5,6},{6,7},{7,8},{8,9},{9,10},{10,1... | collective-permute-start | bytes 589832 | tf_op jit(solution)/shard_map/ppermute | solution.py:15
  50.0 42.0 %collective-permute-start.2 = (bf16[128,768]{0,1:T(8,128)(2,1)}, bf16[128,768]{0,1:T(8,128)(2,1)}, u32[]{:S(2)}, u32[]{:S(2)}) collective-permute-start(bf16[128,768]{0,1:T(8,128)(2,1)} %bitcast.2), channel_id=1, source_target_pairs={{0,2},{1,3},{2,4},{3,5},{4,6},{5,7},{6,8},{7,9},{8,10},{9,11},{10,... | collective-permute-start | bytes 589832 | tf_op jit(solution)/shard_map/ppermute | solution.py:15
  60.6 28.8 %collective-permute-start.1 = (bf16[128,768]{0,1:T(8,128)(2,1)}, bf16[128,768]{0,1:T(8,128)(2,1)}, u32[]{:S(2)}, u32[]{:S(2)}) collective-permute-start(bf16[128,768]{0,1:T(8,128)(2,1)} %bitcast.2), channel_id=1, source_target_pairs={{0,3},{1,4},{2,5},{3,6},{4,7},{5,8},{6,9},{7,10},{8,11},{9,12},{10... | collective-permute-start | bytes 589832 | tf_op jit(solution)/shard_map/ppermute | solution.py:15
  64.2 21.9 %collective-permute-start = (bf16[128,768]{0,1:T(8,128)(2,1)}, bf16[128,768]{0,1:T(8,128)(2,1)}, u32[]{:S(2)}, u32[]{:S(2)}) collective-permute-start(bf16[128,768]{0,1:T(8,128)(2,1)} %bitcast.2), channel_id=1, source_target_pairs={{0,4},{1,5},{2,6},{3,7},{4,8},{5,9},{6,10},{7,11},{8,12},{9,13},{1... | collective-permute-start | bytes 589832 | tf_op jit(solution)/shard_map/ppermute | solution.py:15
  152.8 14.2 %copy-start.31 = (bf16[128,4,64]{0,2,1:T(8,128)(2,1)S(1)}, bf16[128,4,64]{0,2,1:T(8,128)(2,1)}, u32[]{:S(2)}) copy-start(bf16[128,4,64]{0,2,1:T(8,128)(2,1)} %fusion.60) | copy-start | bytes 196612
  152.8 14.2 %copy-start.21 = (f32[128,4,64]{0,2,1:T(8,128)S(1)}, f32[128,4,64]{0,2,1:T(8,128)}, u32[]{:S(2)}) copy-start(f32[128,4,64]{0,2,1:T(8,128)} %fusion.55) | copy-start | bytes 393220
  152.8 14.2 %copy-start.22 = (f32[128,4,64]{0,2,1:T(8,128)S(1)}, f32[128,4,64]{0,2,1:T(8,128)}, u32[]{:S(2)}) copy-start(f32[128,4,64]{0,2,1:T(8,128)} %fusion.52) | copy-start | bytes 393220
  153.1 24.8 %collective-permute-start.15 = (f32[128,768]{0,1:T(8,128)S(1)}, f32[128,768]{0,1:T(8,128)S(1)}, u32[]{:S(2)}, u32[]{:S(2)}) collective-permute-start(f32[128,768]{0,1:T(8,128)S(1)} %bitcast.121), channel_id=1, source_target_pairs={{4,0},{5,1},{6,2},{7,3},{8,4},{9,5},{10,6},{11,7},{12,8},{13,9},{1... | collective-permute-start | bytes 1179656 | tf_op jit(solution)/shard_map/ppermute | solution.py:15
  156.7 41.5 %collective-permute-start.13 = (f32[128,768]{0,1:T(8,128)S(1)}, f32[128,768]{0,1:T(8,128)S(1)}, u32[]{:S(2)}, u32[]{:S(2)}) collective-permute-start(f32[128,768]{0,1:T(8,128)S(1)} %bitcast.120), channel_id=1, source_target_pairs={{2,0},{3,1},{4,2},{5,3},{6,4},{7,5},{8,6},{9,7},{10,8},{11,9},{12,... | collective-permute-start | bytes 1179656 | tf_op jit(solution)/shard_map/ppermute | solution.py:15
  161.2 56.9 %collective-permute-start.14 = (f32[128,768]{0,1:T(8,128)S(1)}, f32[128,768]{0,1:T(8,128)S(1)}, u32[]{:S(2)}, u32[]{:S(2)}) collective-permute-start(f32[128,768]{0,1:T(8,128)S(1)} %bitcast.119), channel_id=1, source_target_pairs={{3,0},{4,1},{5,2},{6,3},{7,4},{8,5},{9,6},{10,7},{11,8},{12,9},{13... | collective-permute-start | bytes 1179656 | tf_op jit(solution)/shard_map/ppermute | solution.py:15
  163.1 85.5 %collective-permute-start.12 = (f32[128,768]{0,1:T(8,128)S(1)}, f32[128,768]{0,1:T(8,128)S(1)}, u32[]{:S(2)}, u32[]{:S(2)}) collective-permute-start(f32[128,768]{0,1:T(8,128)S(1)} %bitcast.118), channel_id=1, source_target_pairs={{1,0},{2,1},{3,2},{4,3},{5,4},{6,5},{7,6},{8,7},{9,8},{10,9},{11,1... | collective-permute-start | bytes 1179656 | tf_op jit(solution)/shard_map/ppermute | solution.py:15
  165.1 84.2 %collective-permute-start.11 = (f32[128,768]{0,1:T(8,128)S(1)}, f32[128,768]{0,1:T(8,128)S(1)}, u32[]{:S(2)}, u32[]{:S(2)}) collective-permute-start(f32[128,768]{0,1:T(8,128)S(1)} %bitcast.117), channel_id=1, source_target_pairs={{4,0},{5,1},{6,2},{7,3},{8,4},{9,5},{10,6},{11,7},{12,8},{13,9},{1... | collective-permute-start | bytes 1179656 | tf_op jit(solution)/shard_map/ppermute | solution.py:15
  177.9 88.5 %collective-permute-start.9 = (f32[128,768]{0,1:T(8,128)S(1)}, f32[128,768]{0,1:T(8,128)S(1)}, u32[]{:S(2)}, u32[]{:S(2)}) collective-permute-start(f32[128,768]{0,1:T(8,128)S(1)} %bitcast.116), channel_id=1, source_target_pairs={{2,0},{3,1},{4,2},{5,3},{6,4},{7,5},{8,6},{9,7},{10,8},{11,9},{12,... | collective-permute-start | bytes 1179656 | tf_op jit(solution)/shard_map/ppermute | solution.py:15
  198.1 87.0 %collective-permute-start.10 = (f32[128,768]{0,1:T(8,128)S(1)}, f32[128,768]{0,1:T(8,128)S(1)}, u32[]{:S(2)}, u32[]{:S(2)}) collective-permute-start(f32[128,768]{0,1:T(8,128)S(1)} %bitcast.115), channel_id=1, source_target_pairs={{3,0},{4,1},{5,2},{6,3},{7,4},{8,5},{9,6},{10,7},{11,8},{12,9},{13... | collective-permute-start | bytes 1179656 | tf_op jit(solution)/shard_map/ppermute | solution.py:15
  218.1 75.3 %collective-permute-start.8 = (f32[128,768]{0,1:T(8,128)S(1)}, f32[128,768]{0,1:T(8,128)S(1)}, u32[]{:S(2)}, u32[]{:S(2)}) collective-permute-start(f32[128,768]{0,1:T(8,128)S(1)} %bitcast.114), channel_id=1, source_target_pairs={{1,0},{2,1},{3,2},{4,3},{5,4},{6,5},{7,6},{8,7},{9,8},{10,9},{11,1... | collective-permute-start | bytes 1179656 | tf_op jit(solution)/shard_map/ppermute | solution.py:15
  249.2 44.4 %copy-start.18 = (f32[128,32]{0,1:T(8,128)S(1)}, f32[128,32]{0,1:T(8,128)}, u32[]{:S(2)}) copy-start(f32[128,32]{0,1:T(8,128)} %copy-done.17) | copy-start | bytes 49156
  249.2 44.4 %copy-start.20 = (f32[128,32]{0,1:T(8,128)S(1)}, f32[128,32]{0,1:T(8,128)}, u32[]{:S(2)}) copy-start(f32[128,32]{0,1:T(8,128)} %copy-done.19) | copy-start | bytes 49156
  297.3 249.0 %all-gather.3.cloned.1.call-start = ((), (), s32[]{:S(2)}) async-start(), calls=%async_computation.2 | async-start | bytes 1327104 | tf_op jit(solution)/shard_map/all_gather | solution.py:218
  (42 other events, 132.4 us)
Sparse Core Ops, SparseCore 0:
  297.5 221.5 reduce-scatter.1
  520.9 25.4 all-gather.2
